TPU v7x, 128 devices: a whole 4x4x4 slice. The times are simulated.
128 devices in a mesh: lane: 64 (over z, y, x), ctx: 2 (over core).
Axes of the slice: x: 4, y: 4, z: 4, core: 2. Of those that a mesh axis runs over, the one named last changes fastest.
Arguments:
- view_tokens: bfloat16 [64, 2048, 768], P('lane', 'ctx'), may hold values from -6 to 6
- destinations: int32 [64, 128], P('lane', 'ctx'), may hold values from 0 to 63, as said below
- w_query: bfloat16 [768, 768], replicated, may hold values from -0.21875 to 0.21875
- w_key: bfloat16 [768, 768], replicated, may hold values from -0.21875 to 0.21875
- w_value: bfloat16 [768, 768], replicated, may hold values from -0.21875 to 0.21875
- rate_vector: bfloat16 [768], replicated, may hold values from -0.21875 to 0.21875
- fast_gate: bfloat16 [768, 768], replicated, may hold values from -0.21875 to 0.21875
- fast_up: bfloat16 [768, 768], replicated, may hold values from -0.21875 to 0.21875
- fast_down: bfloat16 [768, 768], replicated, may hold values from -0.21875 to 0.21875
- out_gain: float32 [768], replicated, may hold values from 0.1 to 1.9
Outputs:
- ttt_output: bfloat16 [64, 2048, 768], P('lane', 'ctx')
Inputs may be any that keep to these rules, and one draw needn't show every extreme that they name: `destinations`: for every source device and every segment, the 64 entries name every lane once, except that one lane is named twice and one lane not at all; over all source devices of one segment every lane is named exactly 64 times.
All inputs are finite; a program needn't handle non-finite values.
Results may differ from a plain program's by a relative error of at most 0.012.
Values may be sent and summed in bfloat16 or wider, within the bound.
A program may use at most 128 MiB of HBM per device.

v0:
```python
import jax
import jax.numpy as jnp
from jax import lax
from jax.experimental import pallas as pl
from jax.experimental.pallas import tpu as pltpu
from jax.sharding import PartitionSpec as P

MESH = pl.DeviceIdType.MESH
LANES = 64
BLK = 16
SIDE = 4
GROUPS = 4
SPREAD = 21
GATHER = 61
ORDERS = ((2, 1, 0), (0, 2, 1), (1, 0, 2))


def coords_of(lane):
    return (lane // 16, (lane // 4) % 4, lane % 4)


def lane_of(coords):
    return coords[0] * 16 + coords[1] * 4 + coords[2]


def dot_nn(left, right):
    return jnp.dot(left, right, preferred_element_type=jnp.float32)


def dot_nt(left, right):
    return lax.dot_general(left, right, (((1,), (1,)), ((), ())), preferred_element_type=jnp.float32)


def dot_tn(left, right):
    return lax.dot_general(left, right, (((0,), (0,)), ((), ())), preferred_element_type=jnp.float32)


def row_scale(values):
    return lax.rsqrt(jnp.mean(values * values, axis=-1, keepdims=True) + 1e-06)


def spread(row):
    return jnp.broadcast_to(row, (128, 128)).T[:LANES]


def prefix(counts, source):
    upto = counts
    shift = 1
    while shift < LANES:
        upto = upto + jnp.where(source >= shift, pltpu.roll(upto, shift, axis=0), 0)
        shift *= 2
    return upto - counts


def send_rows(dest_row):
    block = lax.broadcasted_iota(jnp.int32, (LANES, 128), 0)
    lane = lax.broadcasted_iota(jnp.int32, (LANES, 128), 1)
    lane_row = lax.broadcasted_iota(jnp.int32, (1, 128), 1)
    named = spread(dest_row) == lane
    count = jnp.sum(named.astype(jnp.int32), axis=0, keepdims=True)
    total = jnp.sum(jnp.where(named, block, 0), axis=0, keepdims=True)
    first = jnp.min(jnp.where(named, block, LANES - 1), axis=0, keepdims=True)

    def of(mask, value):
        return jnp.sum(spread(jnp.where(mask, value, 0)), axis=0, keepdims=True)

    twice = count == 2
    absent = (count == 0) & (lane_row < LANES)
    return first, of(twice, total - first), of(twice, lane_row), of(absent, lane_row)


def order_rows(doubled, missed, me):
    source = lax.broadcasted_iota(jnp.int32, (LANES, 128), 0)
    spot = lax.broadcasted_iota(jnp.int32, (LANES, 128), 1)
    usual = (missed != me).astype(jnp.int32)
    hole = 1 - usual
    double = (doubled == me).astype(jnp.int32)
    start = prefix(usual + double, source)
    hole_rank = prefix(hole, source)
    double_rank = prefix(double, source)
    offset = (
        ((me // 16 - source // 16) % SIDE) * 16
        + ((me // 4 - source // 4) % SIDE) * 4
        + (me - source) % SIDE
    )
    slot = (offset * GATHER) % LANES

    def row(mask, value):
        return jnp.sum(jnp.where(mask, value, 0), axis=0, keepdims=True)

    by_source = row(source == spot, hole_rank)
    filler = (double == 1) & (double_rank == by_source)
    return (
        row(source == spot, usual),
        row(filler, source // 16),
        row(filler, (source // 4) % SIDE),
        row(filler, source % SIDE),
        row((hole == 1) & (hole_rank == spot), slot),
        row((usual == 1) & (start == spot), slot)
        + row((double == 1) & (start + usual == spot), double_rank + LANES),
    )


def scene_kernel(view_hbm, dest_hbm, wq_hbm, wk_hbm, wv_hbm, rate_hbm, gate_hbm, up_hbm, down_hbm, gain_hbm,
                 out_ref, order_ref,
                 view, dest, wq, wk, wv, rate_row, gate, up, down, gain, rate_w,
                 idx_v, idx_s, rows_v, rows_s, send, prim, ext, metas,
                 tokens, queries, keys, values, term, hidden, grad, grad_down, gu_w, down_w,
                 other_gu, other_down, sums, other_sums, result,
                 load_sem, local_sem, send_sem, recv_sem, ext_send, ext_recv, meta_send, meta_recv,
                 key_send, key_recv, val_send, val_recv, sum_send, sum_recv, w_send, w_recv):
    me = lax.axis_index("lane")
    ctx = lax.axis_index("ctx")
    here = coords_of(me)
    mate = (me, 1 - ctx)
    width = tokens.shape[1]
    half = width // 2
    part = width // 3
    chunk = tokens.shape[0] // GROUPS
    blocks = chunk // BLK
    step_size = 0.5 * width ** (-0.5)

    barrier = pltpu.get_barrier_semaphore()

    def greet(k, carry):
        pl.semaphore_signal(barrier, inc=1, device_id=(lax.rem(me + k, LANES), ctx), device_id_type=MESH)
        return carry

    lax.fori_loop(1, LANES, greet, 0)
    pl.semaphore_signal(barrier, inc=1, device_id=mate, device_id_type=MESH)

    loads = [
        pltpu.make_async_copy(a, b, load_sem.at[i])
        for i, (a, b) in enumerate((
            (dest_hbm, dest), (view_hbm, view), (wk_hbm, wk), (wv_hbm, wv), (wq_hbm, wq), (gate_hbm, gate),
            (up_hbm, up), (down_hbm, down), (rate_hbm, rate_row), (gain_hbm, gain)))
    ]
    for copy in loads:
        copy.start()
    loads[0].wait()

    first, second, doubled, missed = send_rows(jnp.concatenate([dest[...], dest[...]], axis=1))
    idx_v[0:1, :] = first
    idx_v[1:2, :] = second
    metas[here[0], here[1], here[2], 0:1, :] = doubled
    metas[here[0], here[1], here[2], 1:2, :] = missed
    to_idx = pltpu.make_async_copy(idx_v, idx_s, local_sem.at[0])
    to_idx.start()
    to_idx.wait()
    loads[1].wait()

    def block_of(b):
        return view[b]

    def peer(k):
        d = coords_of(lax.rem(k * SPREAD, LANES))
        return lane_of([(h + o) % SIDE for h, o in zip(here, d)])

    ext[here[0], here[1], here[2]] = block_of(idx_s[1, 0])
    prim[0] = block_of(idx_s[0, me])

    def pack(k, carry):
        send[k] = block_of(idx_s[0, peer(k)])
        return carry

    lax.fori_loop(1, LANES, pack, 0)
    pl.semaphore_wait(barrier, LANES)

    def stage_copy(ref, tail, order, stage, delta, back, sends, recvs):
        axis = order[stage]
        spot = list(here)
        if back:
            spot[axis] = (here[axis] - delta) % SIDE
        for done in order[:stage]:
            spot[done] = pl.ds(0, SIDE)
        to = list(here)
        to[axis] = (here[axis] + delta) % SIDE
        slab = ref.at[(*spot, *tail)]
        return pltpu.make_async_remote_copy(
            src_ref=slab, dst_ref=slab, send_sem=sends, recv_sem=recvs,
            device_id=(lane_of(to), ctx), device_id_type=MESH)

    def stage_copies(stage, back):
        made = []
        for delta in (1, 3, 2):
            made.append(stage_copy(
                metas, (), ORDERS[0], stage, delta, back,
                meta_send.at[stage, delta - 1], meta_recv.at[stage, delta - 1]))
            for p in range(3):
                made.append(stage_copy(
                    ext, (slice(None), pl.ds(p * part, part)), ORDERS[p], stage, delta, back,
                    ext_send.at[p, stage, delta - 1], ext_recv.at[p, stage, delta - 1]))
        return made

    def start_stage(stage):
        for copy in stage_copies(stage, False):
            copy.start()

    def end_stage(stage):
        for copy in stage_copies(stage, True):
            copy.wait_recv()

    def post(k, carry):
        pltpu.make_async_remote_copy(
            src_ref=send.at[k], dst_ref=prim.at[k],
            send_sem=send_sem, recv_sem=recv_sem.at[k // blocks],
            device_id=(peer(k), ctx), device_id_type=MESH).start()
        return carry

    start_stage(0)
    lax.fori_loop(1, 8, post, 0)
    for copy in loads[2:]:
        copy.wait()
    mine = pl.ds(pl.multiple_of(ctx * half, 128), half)
    gu_w[0, pl.ds(0, half), :] = gate[:, mine].T
    gu_w[0, pl.ds(half, half), :] = up[:, mine].T
    down_w[0] = down[mine, :]
    rate_w[...] = jnp.broadcast_to(rate_row[...].astype(jnp.float32), (128, width)).T.astype(jnp.bfloat16)
    end_stage(0)
    start_stage(1)
    lax.fori_loop(8, 16, post, 0)
    end_stage(1)
    start_stage(2)
    lax.fori_loop(16, LANES, post, 0)
    end_stage(2)

    table = metas[...].reshape(LANES, 2, 128)
    for i, row in enumerate(order_rows(table[:, 0, :], table[:, 1, :], me)):
        rows_v[i:i + 1, :] = row
    to_rows = pltpu.make_async_copy(rows_v, rows_s, local_sem.at[0])
    to_rows.start()
    to_order = pltpu.make_async_copy(rows_v, order_ref, local_sem.at[1])
    to_order.start()
    to_rows.wait()

    def share(ref, sends, recvs, seg, c):
        piece = ref.at[seg, pl.ds(c * chunk, chunk)]
        return pltpu.make_async_remote_copy(
            src_ref=piece, dst_ref=piece, send_sem=sends.at[c], recv_sem=recvs.at[c],
            device_id=mate, device_id_type=MESH)

    def fill(k, carry):
        d = coords_of(lax.rem(k * SPREAD, LANES))
        s = lane_of([(h - o) % SIDE for h, o in zip(here, d)])
        keep = rows_s[0, s].astype(jnp.float32)
        doubled_block = ext[rows_s[1, s], rows_s[2, s], rows_s[3, s]].astype(jnp.float32)
        block = prim[k].astype(jnp.float32) * keep + doubled_block * (1.0 - keep)
        tokens[pl.ds(pl.multiple_of(k * BLK, BLK), BLK), :] = block.astype(jnp.bfloat16)
        return carry

    def landed(lo, count, g):
        piece = prim.at[pl.ds(lo, count)]
        pltpu.make_async_remote_copy(
            src_ref=piece, dst_ref=piece, send_sem=send_sem, recv_sem=recv_sem.at[g],
            device_id=mate, device_id_type=MESH).wait_recv()

    def from_mate(c):
        share(keys, key_send, key_recv, 1 - ctx, c).wait_recv()
        share(values, val_send, val_recv, 1 - ctx, c).wait_recv()

    def terms(seg, c):
        rows = pl.ds(c * chunk, chunk)
        pre = dot_nt(keys[seg, rows, :], gu_w[seg])
        back = dot_nt(values[seg, rows, :], down_w[seg])
        gate_pre, up_pre = pre[:, :half], pre[:, half:]
        gate_sig = jax.nn.sigmoid(gate_pre)
        gated = gate_pre * gate_sig
        hidden[rows, :] = (gated * up_pre).astype(jnp.bfloat16)
        term[rows, pl.ds(0, half)] = (
            back * up_pre * gate_sig * (1.0 + gate_pre * (1.0 - gate_sig))
        ).astype(jnp.bfloat16)
        term[rows, pl.ds(half, half)] = (back * gated).astype(jnp.bfloat16)

    def first_terms(c):
        @pl.when(ctx == 1)
        def _():
            from_mate(c)

        terms(0, c)

    def project(c, carry):
        @pl.when(c == 0)
        def _():
            landed(1, blocks - 1, 0)

        @pl.when(c > 0)
        def _():
            landed(c * blocks, blocks, c)

        lax.fori_loop(c * blocks, (c + 1) * blocks, fill, 0)
        rows = pl.ds(c * chunk, chunk)
        x = tokens[rows, :]
        k = dot_nn(x, wk[...])
        keys[ctx, rows, :] = (k * row_scale(k)).astype(jnp.bfloat16)
        share(keys, key_send, key_recv, ctx, c).start()
        rate = dot_nn(x, rate_w[...])
        rate = jnp.maximum(rate, 0.0) + jnp.log1p(jnp.exp(-jnp.abs(rate)))
        v = dot_nn(x, wv[...])
        values[ctx, rows, :] = (rate[:, :1] * v).astype(jnp.bfloat16)
        share(values, val_send, val_recv, ctx, c).start()
        q = dot_nn(x, wq[...])
        queries[rows, :] = (q * row_scale(q)).astype(jnp.bfloat16)

        @pl.when(c > 0)
        def _():
            first_terms(c - 1)

        return carry

    lax.fori_loop(0, GROUPS, project, 0)
    first_terms(GROUPS - 1)

    def share_sums(seg):
        return pltpu.make_async_remote_copy(
            src_ref=sums.at[seg], dst_ref=other_sums.at[seg], send_sem=sum_send.at[seg], recv_sem=sum_recv.at[seg],
            device_id=mate, device_id_type=MESH)

    def share_weights(seg):
        return (
            pltpu.make_async_remote_copy(
                src_ref=gu_w.at[seg + 1], dst_ref=other_gu, send_sem=w_send.at[0], recv_sem=w_recv.at[0],
                device_id=mate, device_id_type=MESH),
            pltpu.make_async_remote_copy(
                src_ref=down_w.at[seg + 1], dst_ref=other_down, send_sem=w_send.at[1], recv_sem=w_recv.at[1],
                device_id=mate, device_id_type=MESH),
        )

    def renew(seg):
        def slopes(j, carry):
            cols = pl.ds(pl.multiple_of(j * half, 128), half)
            g = dot_tn(term[:, cols], keys[seg])
            grad[pl.ds(j * half, half), :] = g
            sums[seg, pl.ds(j, 1), :] = jnp.sum(g * g, axis=0, keepdims=True)
            return carry

        lax.fori_loop(0, 2, slopes, 0)
        share_sums(seg).start()
        grad_down[...] = dot_tn(hidden[...], values[seg])
        g = grad_down[...]
        down_w[seg + 1] = (
            down_w[seg].astype(jnp.float32) + step_size * g * row_scale(g)
        ).astype(jnp.bfloat16)
        share_sums(seg).wait_recv()
        for j in range(2):
            rows = pl.ds(j * half, half)
            total = sums[seg, pl.ds(j, 1), :] + other_sums[seg, pl.ds(j, 1), :]
            scale = step_size * lax.rsqrt(total * (1.0 / width) + 1e-06)
            gu_w[seg + 1, rows, :] = (
                gu_w[seg, rows, :].astype(jnp.float32) + grad[rows, :] * scale
            ).astype(jnp.bfloat16)

    renew(0)

    @pl.when(ctx == 1)
    def _():
        for copy in share_weights(0):
            copy.start()

    @pl.when(ctx == 0)
    def _():
        def one(c, carry):
            from_mate(c)
            return carry

        lax.fori_loop(0, GROUPS, one, 0)

    def second_terms(c, carry):
        terms(1, c)
        return carry

    lax.fori_loop(0, GROUPS, second_terms, 0)
    renew(1)

    @pl.when(ctx == 0)
    def _():
        for copy in share_weights(1):
            copy.start()

    def answer_half(rows, gu):
        pre = dot_nt(queries[rows, :], gu)
        q_gate, q_up = pre[:, :half], pre[:, half:]
        return (q_gate * jax.nn.sigmoid(q_gate) * q_up).astype(jnp.bfloat16)

    def answer_own(c, carry):
        rows = pl.ds(c * chunk, chunk)
        hidden[rows, :] = answer_half(rows, gu_w[ctx + 1])
        return carry

    lax.fori_loop(0, GROUPS, answer_own, 0)
    for copy in share_weights(0):
        copy.wait_recv()

    def out_copy(c):
        rows = pl.ds(c * chunk, chunk)
        return pltpu.make_async_copy(result.at[rows], out_ref.at[rows], load_sem.at[c])

    def answer(c, carry):
        rows = pl.ds(c * chunk, chunk)
        y = dot_nn(hidden[rows, :], down_w[ctx + 1])
        y = y + dot_nn(answer_half(rows, other_gu[...]), other_down[...])
        result[rows, :] = (y * row_scale(y) * gain[...]).astype(jnp.bfloat16)
        out_copy(c).start()
        return carry

    lax.fori_loop(0, GROUPS, answer, 0)

    def sent(c, carry):
        share(keys, key_send, key_recv, ctx, c).wait_send()
        share(values, val_send, val_recv, ctx, c).wait_send()
        out_copy(c).wait()
        return carry

    lax.fori_loop(0, GROUPS, sent, 0)
    for seg in range(2):
        share_sums(seg).wait_send()
    for copy in share_weights(0):
        copy.wait_send()
    for stage in range(3):
        for copy in stage_copies(stage, False):
            copy.wait_send()
    to_order.wait()
    piece = send.at[pl.ds(1, LANES - 1)]
    pltpu.make_async_remote_copy(
        src_ref=piece, dst_ref=piece, send_sem=send_sem, recv_sem=recv_sem.at[0],
        device_id=mate, device_id_type=MESH).wait_send()


def scene(*operands):
    width = operands[0].shape[2]
    rows = LANES * BLK
    half = width // 2
    any_ = pl.BlockSpec(memory_space=pl.ANY)
    bf, f32, i32, dma, vmem = jnp.bfloat16, jnp.float32, jnp.int32, pltpu.SemaphoreType.DMA, pltpu.VMEM
    square = vmem((width, width), bf)
    return pl.pallas_call(
        scene_kernel,
        out_shape=(jax.ShapeDtypeStruct((rows, width), bf), jax.ShapeDtypeStruct((8, 128), i32)),
        in_specs=[any_] * len(operands),
        out_specs=(any_, any_),
        scratch_shapes=[
            vmem((LANES, BLK, width), bf), vmem((1, LANES), i32), square, square, square, vmem((1, width), bf),
            square, square, square, vmem((1, width), f32), vmem((width, 128), bf),
            vmem((8, 128), i32), pltpu.SMEM((8, 128), i32), vmem((8, 128), i32), pltpu.SMEM((8, 128), i32),
            vmem((LANES, BLK, width), bf), vmem((LANES, BLK, width), bf),
            vmem((SIDE, SIDE, SIDE, BLK, width), bf), vmem((SIDE, SIDE, SIDE, 2, 128), i32),
            vmem((rows, width), bf), vmem((rows, width), bf),
            vmem((2, rows, width), bf), vmem((2, rows, width), bf), vmem((rows, width), bf), vmem((rows, half), bf),
            vmem((width, width), f32), vmem((half, width), f32),
            vmem((3, width, width), bf), vmem((3, half, width), bf),
            square, vmem((half, width), bf), vmem((2, 8, width), f32), vmem((2, 8, width), f32), vmem((rows, width), bf),
            dma((10,)), dma((2,)), dma, dma((GROUPS,)),
            dma((3, 3, 3)), dma((3, 3, 3)), dma((3, 3)), dma((3, 3)),
            dma((4,)), dma((4,)), dma((4,)), dma((4,)), dma((2,)), dma((2,)), dma((2,)), dma((2,)),
        ],
        compiler_params=pltpu.CompilerParams(
            collective_id=0, has_side_effects=True, vmem_limit_bytes=60 << 20
        ),
        name="scene",
    )(*operands)


def settle_kernel(order_ref, blocks_ref, out_ref, sem):
    def move(r, carry):
        code = order_ref[5, r]
        slot = jnp.where(code < LANES, code, order_ref[4, jnp.maximum(code - LANES, 0)])
        pltpu.make_async_copy(blocks_ref.at[slot], out_ref.at[r], sem).start()
        return carry

    lax.fori_loop(0, LANES, move, 0)
    pltpu.make_async_copy(blocks_ref, out_ref, sem).wait()


def settle(order, blocks):
    return pl.pallas_call(
        settle_kernel,
        out_shape=jax.ShapeDtypeStruct(blocks.shape, blocks.dtype),
        in_specs=[pl.BlockSpec(memory_space=pltpu.SMEM), pl.BlockSpec(memory_space=pl.ANY)],
        out_specs=pl.BlockSpec(memory_space=pl.ANY),
        scratch_shapes=[pltpu.SemaphoreType.DMA],
        name="settle",
    )(order, blocks)


def body(view_tokens, destinations, w_query, w_key, w_value, rate_vector, fast_gate, fast_up, fast_down, out_gain):
    width = view_tokens.shape[2]
    slots, order = scene(
        view_tokens.reshape(LANES, BLK, width), destinations, w_query, w_key, w_value, rate_vector[None, :],
        fast_gate, fast_up, fast_down, out_gain[None, :]
    )
    out = settle(order, slots.reshape(LANES, BLK, width))
    return out.reshape(1, LANES * BLK, width)


def solution(mesh):
    placed = (P("lane", "ctx", None), P("lane", "ctx"), P(), P(), P(), P(), P(), P(), P(), P())
    return jax.shard_map(
        body, mesh=mesh, in_specs=placed, out_specs=P("lane", "ctx", None), check_vma=False
    )
```

profile of v0, /device:TPU:29, one launch (start us, length us, event | category | flops | bytes accessed | tf_op | source)
XLA Modules:
  0.0 122.9 jit_solution(2213676604671211960)
XLA Ops:
  0.0 1.3 %broadcast_in_dim.6.rate_hbm = bf16[1,768]{1,0:T(2,128)(2,1)} reshape(bf16[768]{0:T(1024)(128)(2,1)} %param.15) | data formatting | bytes 3072 | tf_op jit(solution)/shard_map/broadcast_in_dim | solution.py:487
  1.3 1.3 %broadcast_in_dim.7.gain_hbm = f32[1,768]{1,0:T(1,128)} reshape(f32[768]{0:T(1024)} %param.19) | data formatting | bytes 6144 | tf_op jit(solution)/shard_map/broadcast_in_dim | solution.py:488
  2.5 70.9 %scene.1 = (bf16[1024,768]{1,0:T(8,128)(2,1)}, s32[8,128]{1,0:T(8,128)}) custom-call(bf16[64,16,768]{2,1,0:T(8,128)(2,1)} %bitcast.3, s32[1,64]{1,0:T(1,128)} %dest_hbm.1, bf16[768,768]{1,0:T(8,128)(2,1)} %wq_hbm.1, bf16[768,768]{1,0:T(8,128)(2,1)} %wk_hbm.1, bf16[768,768]{1,0:T(8,128)(2,1)} %wv_hbm.1, bf16[1,768]{1,0:T(2,128)(2,1)} %broadcast_in_dim.6.rate_hbm, ...), custom_call_target="tpu_custom_call" | custom-call | tf_op jit(solution)/shard_map/scene/pallas_call | solution.py:435
  73.4 49.5 %settle.1 = bf16[64,16,768]{2,1,0:T(8,128)(2,1)} custom-call(s32[8,128]{1,0:T(8,128)} %get-tuple-element.7.order_ref, bf16[64,16,768]{2,1,0:T(8,128)(2,1)} %bitcast.4), custom_call_target="tpu_custom_call" | custom-call | tf_op jit(solution)/shard_map/settle/pallas_call | solution.py:474
where the time goes:
time: 123 us
  Pallas kernels  120 us (98%)
  local copies, waits for them, and re-layouts  2.52 us (2%)
    pallas_call x1, Pallas kernels, scene(): pl.pallas_call(scene_kernel, out_shape=(jax.ShapeDtypeStruct((rows, width...  70.9 us
    pallas_call x1, Pallas kernels, settle(): pl.pallas_call(settle_kernel, out_shape=jax.ShapeDtypeStruct(blocks.shape...  49.5 us

commit v1 on v0

--- a/solution.py
+++ b/solution.py
@@ -474,7 +474,7 @@
     return pl.pallas_call(
         settle_kernel,
         out_shape=jax.ShapeDtypeStruct(blocks.shape, blocks.dtype),
-        in_specs=[pl.BlockSpec(memory_space=pltpu.SMEM), pl.BlockSpec(memory_space=pl.ANY)],
+        in_specs=[pl.BlockSpec(memory_space=pltpu.SMEM), pl.BlockSpec(memory_space=pltpu.VMEM)],
         out_specs=pl.BlockSpec(memory_space=pl.ANY),
         scratch_shapes=[pltpu.SemaphoreType.DMA],
         name="settle",

time: 123 us -> 76.5 us (0.62)
  Pallas kernels: 120 us -> 73.8 us
    pallas_call x1, Pallas kernels: 49.5 us -> 2.91 us  [settle(): pl.pallas_call(settle_kernel, out_shape=jax.ShapeDtypeStruct(blocks.shape...]
where the time goes in v1:
time: 76.5 us; the launch traced here: 76.3 us
  Pallas kernels  73.8 us (96%)
  local copies, waits for them, and re-layouts  2.52 us (3%)
    pallas_call x1, Pallas kernels, scene(): pl.pallas_call(scene_kernel, out_shape=(jax.ShapeDtypeStruct((rows, width...  70.9 us
    pallas_call x1, Pallas kernels, settle(): pl.pallas_call(settle_kernel, out_shape=jax.ShapeDtypeStruct(blocks.shape...  2.91 us

profile of v1, /device:TPU:29, one launch (start us, length us, event | category | flops | bytes accessed | tf_op | source)
XLA Modules:
  0.0 76.3 jit_solution(12279462426050374703)
XLA Ops:
  0.0 1.3 %broadcast_in_dim.6.rate_hbm = bf16[1,768]{1,0:T(2,128)(2,1)} reshape(bf16[768]{0:T(1024)(128)(2,1)} %param.15) | data formatting | bytes 3072 | tf_op jit(solution)/shard_map/broadcast_in_dim | solution.py:487
  1.3 1.3 %broadcast_in_dim.7.gain_hbm = f32[1,768]{1,0:T(1,128)} reshape(f32[768]{0:T(1024)} %param.19) | data formatting | bytes 6144 | tf_op jit(solution)/shard_map/broadcast_in_dim | solution.py:488
  2.5 70.9 %scene.1 = (bf16[1024,768]{1,0:T(8,128)(2,1)}, s32[8,128]{1,0:T(8,128)}) custom-call(bf16[64,16,768]{2,1,0:T(8,128)(2,1)} %bitcast.3, s32[1,64]{1,0:T(1,128)} %dest_hbm.1, bf16[768,768]{1,0:T(8,128)(2,1)} %wq_hbm.1, bf16[768,768]{1,0:T(8,128)(2,1)} %wk_hbm.1, bf16[768,768]{1,0:T(8,128)(2,1)} %wv_hbm.1, bf16[1,768]{1,0:T(2,128)(2,1)} %broadcast_in_dim.6.rate_hbm, ...), custom_call_target="tpu_custom_call" | custom-call | tf_op jit(solution)/shard_map/scene/pallas_call | solution.py:435
  73.4 2.9 %settle.1 = bf16[64,16,768]{2,1,0:T(8,128)(2,1)} custom-call(s32[8,128]{1,0:T(8,128)} %get-tuple-element.7.order_ref, bf16[64,16,768]{2,1,0:T(8,128)(2,1)} %bitcast.4), custom_call_target="tpu_custom_call" | custom-call | tf_op jit(solution)/shard_map/settle/pallas_call | solution.py:474

commit v2 on v1

--- a/solution.py
+++ b/solution.py
@@ -209,19 +209,19 @@
 
     start_stage(0)
     lax.fori_loop(1, 8, post, 0)
+    end_stage(0)
+    start_stage(1)
+    lax.fori_loop(8, 16, post, 0)
+    end_stage(1)
+    start_stage(2)
+    lax.fori_loop(16, LANES, post, 0)
     for copy in loads[2:]:
         copy.wait()
     mine = pl.ds(pl.multiple_of(ctx * half, 128), half)
     gu_w[0, pl.ds(0, half), :] = gate[:, mine].T
     gu_w[0, pl.ds(half, half), :] = up[:, mine].T
     down_w[0] = down[mine, :]
-    rate_w[...] = jnp.broadcast_to(rate_row[...].astype(jnp.float32), (128, width)).T.astype(jnp.bfloat16)
-    end_stage(0)
-    start_stage(1)
-    lax.fori_loop(8, 16, post, 0)
-    end_stage(1)
-    start_stage(2)
-    lax.fori_loop(16, LANES, post, 0)
+    rate_w[...] = jnp.broadcast_to(rate_row[...].astype(jnp.float32).reshape(1, width), (128, width)).T.astype(jnp.bfloat16)
     end_stage(2)
 
     table = metas[...].reshape(LANES, 2, 128)
@@ -398,7 +398,7 @@
         rows = pl.ds(c * chunk, chunk)
         y = dot_nn(hidden[rows, :], down_w[ctx + 1])
         y = y + dot_nn(answer_half(rows, other_gu[...]), other_down[...])
-        result[rows, :] = (y * row_scale(y) * gain[...]).astype(jnp.bfloat16)
+        result[rows, :] = (y * row_scale(y) * gain[...].reshape(1, width)).astype(jnp.bfloat16)
         out_copy(c).start()
         return carry
 
@@ -438,8 +438,8 @@
         in_specs=[any_] * len(operands),
         out_specs=(any_, any_),
         scratch_shapes=[
-            vmem((LANES, BLK, width), bf), vmem((1, LANES), i32), square, square, square, vmem((1, width), bf),
-            square, square, square, vmem((1, width), f32), vmem((width, 128), bf),
+            vmem((LANES, BLK, width), bf), vmem((1, LANES), i32), square, square, square, vmem((width,), bf),
+            square, square, square, vmem((width,), f32), vmem((width, 128), bf),
             vmem((8, 128), i32), pltpu.SMEM((8, 128), i32), vmem((8, 128), i32), pltpu.SMEM((8, 128), i32),
             vmem((LANES, BLK, width), bf), vmem((LANES, BLK, width), bf),
             vmem((SIDE, SIDE, SIDE, BLK, width), bf), vmem((SIDE, SIDE, SIDE, 2, 128), i32),
@@ -484,8 +484,8 @@
 def body(view_tokens, destinations, w_query, w_key, w_value, rate_vector, fast_gate, fast_up, fast_down, out_gain):
     width = view_tokens.shape[2]
     slots, order = scene(
-        view_tokens.reshape(LANES, BLK, width), destinations, w_query, w_key, w_value, rate_vector[None, :],
-        fast_gate, fast_up, fast_down, out_gain[None, :]
+        view_tokens.reshape(LANES, BLK, width), destinations, w_query, w_key, w_value, rate_vector,
+        fast_gate, fast_up, fast_down, out_gain
     )
     out = settle(order, slots.reshape(LANES, BLK, width))
     return out.reshape(1, LANES * BLK, width)

time: 76.5 us -> 73.3 us (0.958)
  the two profiles are of different devices: /device:TPU:29 before, /device:TPU:61 now
where the time goes in v2:
time: 73.3 us; the launch traced here: 73.1 us
  Pallas kernels  73.1 us (100%)
    pallas_call x1, Pallas kernels, scene(): pl.pallas_call(scene_kernel, out_shape=(jax.ShapeDtypeStruct((rows, width...  70.2 us
    pallas_call x1, Pallas kernels, settle(): pl.pallas_call(settle_kernel, out_shape=jax.ShapeDtypeStruct(blocks.shape...  2.91 us

profile of v2, /device:TPU:61, one launch (start us, length us, event | category | flops | bytes accessed | tf_op | source)
XLA Modules:
  0.0 73.1 jit_solution(9946172160566593822)
XLA Ops:
  0.0 70.2 %scene.1 = (bf16[1024,768]{1,0:T(8,128)(2,1)}, s32[8,128]{1,0:T(8,128)}) custom-call(bf16[64,16,768]{2,1,0:T(8,128)(2,1)} %bitcast.3, s32[1,64]{1,0:T(1,128)} %dest_hbm.1, bf16[768,768]{1,0:T(8,128)(2,1)} %wq_hbm.1, bf16[768,768]{1,0:T(8,128)(2,1)} %wk_hbm.1, bf16[768,768]{1,0:T(8,128)(2,1)} %wv_hbm.1, bf16[768]{0:T(1024)(128)(2,1)} %rate_hbm.1, ...), custom_call_target="tpu_custom_call" | custom-call | tf_op jit(solution)/shard_map/scene/pallas_call | solution.py:435
  70.2 2.9 %settle.1 = bf16[64,16,768]{2,1,0:T(8,128)(2,1)} custom-call(s32[8,128]{1,0:T(8,128)} %get-tuple-element.7.order_ref, bf16[64,16,768]{2,1,0:T(8,128)(2,1)} %bitcast.4), custom_call_target="tpu_custom_call" | custom-call | tf_op jit(solution)/shard_map/settle/pallas_call | solution.py:474

commit v3 on v2

--- a/solution.py
+++ b/solution.py
@@ -10,8 +10,6 @@
 BLK = 16
 SIDE = 4
 GROUPS = 4
-SPREAD = 21
-GATHER = 61
 ORDERS = ((2, 1, 0), (0, 2, 1), (1, 0, 2))
 
 
@@ -37,6 +35,11 @@
 
 def row_scale(values):
     return lax.rsqrt(jnp.mean(values * values, axis=-1, keepdims=True) + 1e-06)
+
+
+def offset_of(k):
+    dz, dy = (k // 4) % SIDE, k % SIDE
+    return dz, dy, (k // 16 + 2 * SIDE - dz - dy) % SIDE
 
 
 def spread(row):
@@ -78,12 +81,8 @@
     start = prefix(usual + double, source)
     hole_rank = prefix(hole, source)
     double_rank = prefix(double, source)
-    offset = (
-        ((me // 16 - source // 16) % SIDE) * 16
-        + ((me // 4 - source // 4) % SIDE) * 4
-        + (me - source) % SIDE
-    )
-    slot = (offset * GATHER) % LANES
+    dz, dy, dx = (me // 16 - source // 16) % SIDE, (me // 4 - source // 4) % SIDE, (me - source) % SIDE
+    slot = ((dz + dy + dx) % SIDE) * 16 + dz * 4 + dy
 
     def row(mask, value):
         return jnp.sum(jnp.where(mask, value, 0), axis=0, keepdims=True)
@@ -153,7 +152,7 @@
         return view[b]
 
     def peer(k):
-        d = coords_of(lax.rem(k * SPREAD, LANES))
+        d = offset_of(k)
         return lane_of([(h + o) % SIDE for h, o in zip(here, d)])
 
     ext[here[0], here[1], here[2]] = block_of(idx_s[1, 0])
@@ -208,13 +207,11 @@
         return carry
 
     start_stage(0)
-    lax.fori_loop(1, 8, post, 0)
+    lax.fori_loop(1, blocks, post, 0)
     end_stage(0)
     start_stage(1)
-    lax.fori_loop(8, 16, post, 0)
     end_stage(1)
     start_stage(2)
-    lax.fori_loop(16, LANES, post, 0)
     for copy in loads[2:]:
         copy.wait()
     mine = pl.ds(pl.multiple_of(ctx * half, 128), half)
@@ -223,7 +220,7 @@
     down_w[0] = down[mine, :]
     rate_w[...] = jnp.broadcast_to(rate_row[...].astype(jnp.float32).reshape(1, width), (128, width)).T.astype(jnp.bfloat16)
     end_stage(2)
-
+    lax.fori_loop(blocks, LANES, post, 0)
     table = metas[...].reshape(LANES, 2, 128)
     for i, row in enumerate(order_rows(table[:, 0, :], table[:, 1, :], me)):
         rows_v[i:i + 1, :] = row
@@ -240,7 +237,7 @@
             device_id=mate, device_id_type=MESH)
 
     def fill(k, carry):
-        d = coords_of(lax.rem(k * SPREAD, LANES))
+        d = offset_of(k)
         s = lane_of([(h - o) % SIDE for h, o in zip(here, d)])
         keep = rows_s[0, s].astype(jnp.float32)
         doubled_block = ext[rows_s[1, s], rows_s[2, s], rows_s[3, s]].astype(jnp.float32)

time: 73.3 us -> 71.8 us (0.980)
  the two profiles are of different devices: /device:TPU:61 before, /device:TPU:1 now
where the time goes in v3:
time: 71.8 us; the launch traced here: 71.6 us
  Pallas kernels  71.6 us (100%)
    pallas_call x1, Pallas kernels, scene(): pl.pallas_call(scene_kernel, out_shape=(jax.ShapeDtypeStruct((rows, width...  68.7 us
    pallas_call x1, Pallas kernels, settle(): pl.pallas_call(settle_kernel, out_shape=jax.ShapeDtypeStruct(blocks.shape...  2.91 us

profile of v3, /device:TPU:1, one launch (start us, length us, event | category | flops | bytes accessed | tf_op | source)
XLA Modules:
  0.0 71.6 jit_solution(6395649092558579860)
XLA Ops:
  0.0 68.7 %scene.1 = (bf16[1024,768]{1,0:T(8,128)(2,1)}, s32[8,128]{1,0:T(8,128)}) custom-call(bf16[64,16,768]{2,1,0:T(8,128)(2,1)} %bitcast.3, s32[1,64]{1,0:T(1,128)} %dest_hbm.1, bf16[768,768]{1,0:T(8,128)(2,1)} %wq_hbm.1, bf16[768,768]{1,0:T(8,128)(2,1)} %wk_hbm.1, bf16[768,768]{1,0:T(8,128)(2,1)} %wv_hbm.1, bf16[768]{0:T(1024)(128)(2,1)} %rate_hbm.1, ...), custom_call_target="tpu_custom_call" | custom-call | tf_op jit(solution)/shard_map/scene/pallas_call | solution.py:432
  68.7 2.9 %settle.1 = bf16[64,16,768]{2,1,0:T(8,128)(2,1)} custom-call(s32[8,128]{1,0:T(8,128)} %get-tuple-element.7.order_ref, bf16[64,16,768]{2,1,0:T(8,128)(2,1)} %bitcast.4), custom_call_target="tpu_custom_call" | custom-call | tf_op jit(solution)/shard_map/settle/pallas_call | solution.py:471

commit v4 on v3

--- a/solution.py
+++ b/solution.py
@@ -27,10 +27,6 @@
 
 def dot_nt(left, right):
     return lax.dot_general(left, right, (((1,), (1,)), ((), ())), preferred_element_type=jnp.float32)
-
-
-def dot_tn(left, right):
-    return lax.dot_general(left, right, (((0,), (0,)), ((), ())), preferred_element_type=jnp.float32)
 
 
 def row_scale(values):
@@ -104,7 +100,7 @@
                  out_ref, order_ref,
                  view, dest, wq, wk, wv, rate_row, gate, up, down, gain, rate_w,
                  idx_v, idx_s, rows_v, rows_s, send, prim, ext, metas,
-                 tokens, queries, keys, values, term, hidden, grad, grad_down, gu_w, down_w,
+                 tokens, queries, keys, values, term, hidden, asked, grad, grad_down, gu_w, down_w,
                  other_gu, other_down, sums, other_sums, result,
                  load_sem, local_sem, send_sem, recv_sem, ext_send, ext_recv, meta_send, meta_recv,
                  key_send, key_recv, val_send, val_recv, sum_send, sum_recv, w_send, w_recv):
@@ -256,17 +252,17 @@
         share(values, val_send, val_recv, 1 - ctx, c).wait_recv()
 
     def terms(seg, c):
-        rows = pl.ds(c * chunk, chunk)
-        pre = dot_nt(keys[seg, rows, :], gu_w[seg])
-        back = dot_nt(values[seg, rows, :], down_w[seg])
-        gate_pre, up_pre = pre[:, :half], pre[:, half:]
+        rows = pl.ds(pl.multiple_of(c * chunk, chunk), chunk)
+        pre = dot_nt(gu_w[seg], keys[seg, rows, :])
+        back = dot_nt(down_w[seg], values[seg, rows, :])
+        gate_pre, up_pre = pre[:half], pre[half:]
         gate_sig = jax.nn.sigmoid(gate_pre)
         gated = gate_pre * gate_sig
-        hidden[rows, :] = (gated * up_pre).astype(jnp.bfloat16)
-        term[rows, pl.ds(0, half)] = (
+        hidden[:, rows] = (gated * up_pre).astype(jnp.bfloat16)
+        term[pl.ds(0, half), rows] = (
             back * up_pre * gate_sig * (1.0 + gate_pre * (1.0 - gate_sig))
         ).astype(jnp.bfloat16)
-        term[rows, pl.ds(half, half)] = (back * gated).astype(jnp.bfloat16)
+        term[pl.ds(half, half), rows] = (back * gated).astype(jnp.bfloat16)
 
     def first_terms(c):
         @pl.when(ctx == 1)
@@ -284,7 +280,7 @@
         def _():
             landed(c * blocks, blocks, c)
 
-        lax.fori_loop(c * blocks, (c + 1) * blocks, fill, 0)
+        lax.fori_loop(0, blocks, lambda j, carry: fill(c * blocks + j, carry), 0, unroll=4)
         rows = pl.ds(c * chunk, chunk)
         x = tokens[rows, :]
         k = dot_nn(x, wk[...])
@@ -312,31 +308,38 @@
             src_ref=sums.at[seg], dst_ref=other_sums.at[seg], send_sem=sum_send.at[seg], recv_sem=sum_recv.at[seg],
             device_id=mate, device_id_type=MESH)
 
-    def share_weights(seg):
-        return (
-            pltpu.make_async_remote_copy(
-                src_ref=gu_w.at[seg + 1], dst_ref=other_gu, send_sem=w_send.at[0], recv_sem=w_recv.at[0],
-                device_id=mate, device_id_type=MESH),
-            pltpu.make_async_remote_copy(
-                src_ref=down_w.at[seg + 1], dst_ref=other_down, send_sem=w_send.at[1], recv_sem=w_recv.at[1],
-                device_id=mate, device_id_type=MESH),
-        )
+    def share_weights(seg, which=(0, 1, 2)):
+        made = []
+        for i in which:
+            rows = pl.ds(i * half, half)
+            source, target = (
+                (down_w.at[seg + 1], other_down) if i == 2 else (gu_w.at[seg + 1, rows], other_gu.at[rows]))
+            made.append(pltpu.make_async_remote_copy(
+                src_ref=source, dst_ref=target, send_sem=w_send.at[i], recv_sem=w_recv.at[i],
+                device_id=mate, device_id_type=MESH))
+        return made
+
+    def send_weights(seg, i):
+        @pl.when(ctx == 1 - seg)
+        def _():
+            share_weights(seg, (i,))[0].start()
 
     def renew(seg):
         def slopes(j, carry):
-            cols = pl.ds(pl.multiple_of(j * half, 128), half)
-            g = dot_tn(term[:, cols], keys[seg])
-            grad[pl.ds(j * half, half), :] = g
+            units = pl.ds(pl.multiple_of(j * half, 128), half)
+            g = dot_nn(term[units, :], keys[seg])
+            grad[units, :] = g
             sums[seg, pl.ds(j, 1), :] = jnp.sum(g * g, axis=0, keepdims=True)
             return carry
 
         lax.fori_loop(0, 2, slopes, 0)
         share_sums(seg).start()
-        grad_down[...] = dot_tn(hidden[...], values[seg])
+        grad_down[...] = dot_nn(hidden[...], values[seg])
         g = grad_down[...]
         down_w[seg + 1] = (
             down_w[seg].astype(jnp.float32) + step_size * g * row_scale(g)
         ).astype(jnp.bfloat16)
+        send_weights(seg, 2)
         share_sums(seg).wait_recv()
         for j in range(2):
             rows = pl.ds(j * half, half)
@@ -345,13 +348,9 @@
             gu_w[seg + 1, rows, :] = (
                 gu_w[seg, rows, :].astype(jnp.float32) + grad[rows, :] * scale
             ).astype(jnp.bfloat16)
+            send_weights(seg, j)
 
     renew(0)
-
-    @pl.when(ctx == 1)
-    def _():
-        for copy in share_weights(0):
-            copy.start()
 
     @pl.when(ctx == 0)
     def _():
@@ -368,11 +367,6 @@
     lax.fori_loop(0, GROUPS, second_terms, 0)
     renew(1)
 
-    @pl.when(ctx == 0)
-    def _():
-        for copy in share_weights(1):
-            copy.start()
-
     def answer_half(rows, gu):
         pre = dot_nt(queries[rows, :], gu)
         q_gate, q_up = pre[:, :half], pre[:, half:]
@@ -380,7 +374,7 @@
 
     def answer_own(c, carry):
         rows = pl.ds(c * chunk, chunk)
-        hidden[rows, :] = answer_half(rows, gu_w[ctx + 1])
+        asked[rows, :] = answer_half(rows, gu_w[ctx + 1])
         return carry
 
     lax.fori_loop(0, GROUPS, answer_own, 0)
@@ -393,7 +387,7 @@
 
     def answer(c, carry):
         rows = pl.ds(c * chunk, chunk)
-        y = dot_nn(hidden[rows, :], down_w[ctx + 1])
+        y = dot_nn(asked[rows, :], down_w[ctx + 1])
         y = y + dot_nn(answer_half(rows, other_gu[...]), other_down[...])
         result[rows, :] = (y * row_scale(y) * gain[...].reshape(1, width)).astype(jnp.bfloat16)
         out_copy(c).start()
@@ -441,13 +435,14 @@
             vmem((LANES, BLK, width), bf), vmem((LANES, BLK, width), bf),
             vmem((SIDE, SIDE, SIDE, BLK, width), bf), vmem((SIDE, SIDE, SIDE, 2, 128), i32),
             vmem((rows, width), bf), vmem((rows, width), bf),
-            vmem((2, rows, width), bf), vmem((2, rows, width), bf), vmem((rows, width), bf), vmem((rows, half), bf),
+            vmem((2, rows, width), bf), vmem((2, rows, width), bf), vmem((width, rows), bf), vmem((half, rows), bf),
+            vmem((rows, half), bf),
             vmem((width, width), f32), vmem((half, width), f32),
             vmem((3, width, width), bf), vmem((3, half, width), bf),
             square, vmem((half, width), bf), vmem((2, 8, width), f32), vmem((2, 8, width), f32), vmem((rows, width), bf),
             dma((10,)), dma((2,)), dma, dma((GROUPS,)),
             dma((3, 3, 3)), dma((3, 3, 3)), dma((3, 3)), dma((3, 3)),
-            dma((4,)), dma((4,)), dma((4,)), dma((4,)), dma((2,)), dma((2,)), dma((2,)), dma((2,)),
+            dma((4,)), dma((4,)), dma((4,)), dma((4,)), dma((2,)), dma((2,)), dma((3,)), dma((3,)),
         ],
         compiler_params=pltpu.CompilerParams(
             collective_id=0, has_side_effects=True, vmem_limit_bytes=60 << 20

time: 71.8 us -> 71.1 us (level)
  no operation moved by 1% of the time
where the time goes in v4:
time: 71.1 us; the launch traced here: 71 us
  Pallas kernels  70.9 us (100%)
    pallas_call x1, Pallas kernels, scene(): pl.pallas_call(scene_kernel, out_shape=(jax.ShapeDtypeStruct((rows, width...  68 us
    pallas_call x1, Pallas kernels, settle(): pl.pallas_call(settle_kernel, out_shape=jax.ShapeDtypeStruct(blocks.shape...  2.91 us

profile of v4, /device:TPU:1, one launch (start us, length us, event | category | flops | bytes accessed | tf_op | source)
XLA Modules:
  0.0 71.0 jit_solution(13738333752734137057)
XLA Ops:
  0.0 68.0 %scene.1 = (bf16[1024,768]{1,0:T(8,128)(2,1)}, s32[8,128]{1,0:T(8,128)}) custom-call(bf16[64,16,768]{2,1,0:T(8,128)(2,1)} %bitcast.3, s32[1,64]{1,0:T(1,128)} %dest_hbm.1, bf16[768,768]{1,0:T(8,128)(2,1)} %wq_hbm.1, bf16[768,768]{1,0:T(8,128)(2,1)} %wk_hbm.1, bf16[768,768]{1,0:T(8,128)(2,1)} %wv_hbm.1, bf16[768]{0:T(1024)(128)(2,1)} %rate_hbm.1, ...), custom_call_target="tpu_custom_call" | custom-call | tf_op jit(solution)/shard_map/scene/pallas_call | solution.py:426
  68.0 2.9 %settle.1 = bf16[64,16,768]{2,1,0:T(8,128)(2,1)} custom-call(s32[8,128]{1,0:T(8,128)} %get-tuple-element.7.order_ref, bf16[64,16,768]{2,1,0:T(8,128)(2,1)} %bitcast.4), custom_call_target="tpu_custom_call" | custom-call | tf_op jit(solution)/shard_map/settle/pallas_call | solution.py:466

commit v5 on v4

--- a/solution.py
+++ b/solution.py
@@ -280,7 +280,7 @@
         def _():
             landed(c * blocks, blocks, c)
 
-        lax.fori_loop(0, blocks, lambda j, carry: fill(c * blocks + j, carry), 0, unroll=4)
+        lax.fori_loop(0, blocks, lambda j, carry: fill(c * blocks + j, carry), 0, unroll=16)
         rows = pl.ds(c * chunk, chunk)
         x = tokens[rows, :]
         k = dot_nn(x, wk[...])
@@ -361,10 +361,11 @@
         lax.fori_loop(0, GROUPS, one, 0)
 
     def second_terms(c, carry):
-        terms(1, c)
-        return carry
-
-    lax.fori_loop(0, GROUPS, second_terms, 0)
+        terms(1, 2 * c)
+        terms(1, 2 * c + 1)
+        return carry
+
+    lax.fori_loop(0, GROUPS // 2, second_terms, 0)
     renew(1)
 
     def answer_half(rows, gu):
@@ -373,11 +374,12 @@
         return (q_gate * jax.nn.sigmoid(q_gate) * q_up).astype(jnp.bfloat16)
 
     def answer_own(c, carry):
-        rows = pl.ds(c * chunk, chunk)
-        asked[rows, :] = answer_half(rows, gu_w[ctx + 1])
-        return carry
-
-    lax.fori_loop(0, GROUPS, answer_own, 0)
+        for i in range(2):
+            rows = pl.ds((2 * c + i) * chunk, chunk)
+            asked[rows, :] = answer_half(rows, gu_w[ctx + 1])
+        return carry
+
+    lax.fori_loop(0, GROUPS // 2, answer_own, 0)
     for copy in share_weights(0):
         copy.wait_recv()
 

time: 71.1 us -> 70.3 us (0.989)
    pallas_call x1, Pallas kernels: 68 us -> 67.2 us  [scene(): pl.pallas_call(scene_kernel, out_shape=(jax.ShapeDtypeStruct((rows, width...]
where the time goes in v5:
time: 70.3 us; the launch traced here: 70.2 us
  Pallas kernels  70.2 us (100%)
    pallas_call x1, Pallas kernels, scene(): pl.pallas_call(scene_kernel, out_shape=(jax.ShapeDtypeStruct((rows, width...  67.2 us
    pallas_call x1, Pallas kernels, settle(): pl.pallas_call(settle_kernel, out_shape=jax.ShapeDtypeStruct(blocks.shape...  2.91 us

profile of v5, /device:TPU:1, one launch (start us, length us, event | category | flops | bytes accessed | tf_op | source)
XLA Modules:
  0.0 70.2 jit_solution(11444307103711347234)
XLA Ops:
  0.0 67.2 %scene.1 = (bf16[1024,768]{1,0:T(8,128)(2,1)}, s32[8,128]{1,0:T(8,128)}) custom-call(bf16[64,16,768]{2,1,0:T(8,128)(2,1)} %bitcast.3, s32[1,64]{1,0:T(1,128)} %dest_hbm.1, bf16[768,768]{1,0:T(8,128)(2,1)} %wq_hbm.1, bf16[768,768]{1,0:T(8,128)(2,1)} %wk_hbm.1, bf16[768,768]{1,0:T(8,128)(2,1)} %wv_hbm.1, bf16[768]{0:T(1024)(128)(2,1)} %rate_hbm.1, ...), custom_call_target="tpu_custom_call" | custom-call | tf_op jit(solution)/shard_map/scene/pallas_call | solution.py:428
  67.3 2.9 %settle.1 = bf16[64,16,768]{2,1,0:T(8,128)(2,1)} custom-call(s32[8,128]{1,0:T(8,128)} %get-tuple-element.7.order_ref, bf16[64,16,768]{2,1,0:T(8,128)(2,1)} %bitcast.4), custom_call_target="tpu_custom_call" | custom-call | tf_op jit(solution)/shard_map/settle/pallas_call | solution.py:468

commit v6 on v5

--- a/solution.py
+++ b/solution.py
@@ -387,15 +387,19 @@
         rows = pl.ds(c * chunk, chunk)
         return pltpu.make_async_copy(result.at[rows], out_ref.at[rows], load_sem.at[c])
 
-    def answer(c, carry):
+    def answer_one(c):
         rows = pl.ds(c * chunk, chunk)
         y = dot_nn(asked[rows, :], down_w[ctx + 1])
         y = y + dot_nn(answer_half(rows, other_gu[...]), other_down[...])
         result[rows, :] = (y * row_scale(y) * gain[...].reshape(1, width)).astype(jnp.bfloat16)
         out_copy(c).start()
-        return carry
-
-    lax.fori_loop(0, GROUPS, answer, 0)
+
+    def answer(c, carry):
+        answer_one(2 * c)
+        answer_one(2 * c + 1)
+        return carry
+
+    lax.fori_loop(0, GROUPS // 2, answer, 0)
 
     def sent(c, carry):
         share(keys, key_send, key_recv, ctx, c).wait_send()

time: 70.3 us -> 69.4 us (0.987)
  Pallas kernels: 70.2 us -> 69.3 us
    pallas_call x1, Pallas kernels: 67.2 us -> 66.4 us  [scene(): pl.pallas_call(scene_kernel, out_shape=(jax.ShapeDtypeStruct((rows, width...]
where the time goes in v6:
time: 69.4 us; the launch traced here: 69.3 us
  Pallas kernels  69.3 us (100%)
    pallas_call x1, Pallas kernels, scene(): pl.pallas_call(scene_kernel, out_shape=(jax.ShapeDtypeStruct((rows, width...  66.4 us
    pallas_call x1, Pallas kernels, settle(): pl.pallas_call(settle_kernel, out_shape=jax.ShapeDtypeStruct(blocks.shape...  2.91 us

profile of v6, /device:TPU:1, one launch (start us, length us, event | category | flops | bytes accessed | tf_op | source)
XLA Modules:
  0.0 69.3 jit_solution(9094084178940109119)
XLA Ops:
  0.0 66.4 %scene.1 = (bf16[1024,768]{1,0:T(8,128)(2,1)}, s32[8,128]{1,0:T(8,128)}) custom-call(bf16[64,16,768]{2,1,0:T(8,128)(2,1)} %bitcast.3, s32[1,64]{1,0:T(1,128)} %dest_hbm.1, bf16[768,768]{1,0:T(8,128)(2,1)} %wq_hbm.1, bf16[768,768]{1,0:T(8,128)(2,1)} %wk_hbm.1, bf16[768,768]{1,0:T(8,128)(2,1)} %wv_hbm.1, bf16[768]{0:T(1024)(128)(2,1)} %rate_hbm.1, ...), custom_call_target="tpu_custom_call" | custom-call | tf_op jit(solution)/shard_map/scene/pallas_call | solution.py:432
  66.4 2.9 %settle.1 = bf16[64,16,768]{2,1,0:T(8,128)(2,1)} custom-call(s32[8,128]{1,0:T(8,128)} %get-tuple-element.7.order_ref, bf16[64,16,768]{2,1,0:T(8,128)(2,1)} %bitcast.4), custom_call_target="tpu_custom_call" | custom-call | tf_op jit(solution)/shard_map/settle/pallas_call | solution.py:472
